TPU v7x, 256 devices: a whole 4x4x8 slice. The times are simulated.
256 devices in a mesh: dp: 16 (over x, y), head: 16 (over z, core).
Axes of the slice: x: 4, y: 4, z: 8, core: 2. Of those that a mesh axis runs over, the one named last changes fastest.
Arguments:
- latents: bfloat16 [2048, 512], P('dp'), may hold values from -6 to 6
- targets: bfloat16 [2048, 32768], P('dp', 'head'), may hold values from -6 to 6
- kv_weight: bfloat16 [512, 32768], P(None, 'head'), may hold values from -0.25 to 0.25
- momentum: float32 [512, 16, 2048], P(None, 'head', 'dp'), may hold values from -120 to 120
Outputs:
- momentum_out: float32 [512, 16, 2048], P(None, 'head', 'dp')
- update: float32 [512, 16, 2048], P(None, 'head', 'dp')
All inputs are finite; a program needn't handle non-finite values.
Results may differ from a plain program's by a relative error of at most 0.0003.
The roundings to bfloat16 on the way count: a program that leaves them out, or rounds other values in their place, can miss the bound.
Values may be sent and summed in bfloat16 or wider, within the bound.
A program may use at most 64 MiB of HBM per device.

v0:
```python
import math
import jax
import jax.numpy as jnp
from jax import lax
from jax.sharding import PartitionSpec as P

C = 32768
ITERS = 2
decay_rate = 0.95
linear_coef = 3.4445
square_coef = -4.775
quint_coef = 2.0315
epsilon = 1e-07


def gram_total(iterate):
    local_gram = lax.dot_general(
        iterate, iterate, (((1,), (1,)), ((), ())), precision=lax.Precision.HIGHEST
    )
    return lax.psum(local_gram, ("dp", "head"))


def local(latents, targets, kv_weight, momentum):
    latent_width = momentum.shape[0]
    sub_width = momentum.shape[2]
    total_tokens = latents.shape[0] * lax.axis_size("dp")
    residual = (
        jnp.dot(latents, kv_weight, preferred_element_type=jnp.float32)
        - targets.astype(jnp.float32)
    ).astype(jnp.bfloat16)
    gradient = lax.psum_scatter(
        lax.dot_general(
            residual, latents, (((0,), (0,)), ((), ())), preferred_element_type=jnp.float32
        ),
        "dp",
        scatter_dimension=0,
        tiled=True,
    ).T
    gradient = gradient * (1.0 / math.sqrt(total_tokens))
    previous = momentum.reshape(latent_width, sub_width)
    momentum_new = decay_rate * previous + gradient
    nesterov = gradient + decay_rate * momentum_new
    squares = lax.psum(jnp.sum(nesterov * nesterov), ("dp", "head"))
    inverse = 1.0 / (jnp.sqrt(squares) + epsilon)
    iterate = nesterov * inverse
    gram_matrix = gram_total(iterate)
    for iteration in range(ITERS):
        if iteration > 0:
            gram_matrix = gram_total(iterate)
        polynomial = square_coef * gram_matrix + quint_coef * jnp.dot(
            gram_matrix, gram_matrix, precision=lax.Precision.HIGHEST
        )
        iterate = linear_coef * iterate + jnp.dot(
            polynomial, iterate, precision=lax.Precision.HIGHEST
        )
    update = iterate * math.sqrt(C)
    return (
        momentum_new.reshape(latent_width, 1, sub_width),
        update.reshape(latent_width, 1, sub_width),
    )


def solution(mesh):
    return jax.shard_map(
        local,
        mesh=mesh,
        in_specs=(P("dp", None), P("dp", "head"), P(None, "head"), P(None, "head", "dp")),
        out_specs=(P(None, "head", "dp"), P(None, "head", "dp")),
        check_vma=False,
    )
```

profile of v0, /device:TPU:2, one launch (start us, length us, event | category | flops | bytes accessed | tf_op | source)
XLA Modules:
  0.0 706.9 jit_solution(13692104984853528014)
XLA Ops:
  7.2 0.0 copy-start
  7.2 0.0 reduce-scatter.2.cloned.1.call-start
  7.2 1.5 copy-done
  8.8 4.0 fusion.3
  12.8 0.0 copy-start.2
  12.8 0.0 reduce-scatter.2.cloned.1.call-update
  12.8 0.0 all-reduce.3.cloned.1.call-start
  12.9 0.9 copy-done.2
  13.7 0.1 copy.6
  13.9 84.5 %reduce-scatter.2.cloned.1.call-done = f32[128,512]{1,0:T(8,128)} async-done(((f32[2048,512]{1,0:T(8,128)}), f32[128,512]{1,0:T(8,128)}) %reduce-scatter.2.cloned.1.call-update) | async-done | bytes 262160 | tf_op jit(solution)/shard_map/reduce_scatter | solution.py:31
  98.3 1.6 multiply_reduce_fusion
  99.9 73.7 %psum.21 = f32[]{:T(128)} all-reduce(f32[]{:T(128)} %get-tuple-element.4), channel_id=1, replica_groups=mesh['dp'=16,'head'=16] {'dp','head'}, use_global_device_ids=true, to_apply=%region_2.0 | all-reduce | flops 1 | bytes 8 | tf_op jit(solution)/shard_map/psum | solution.py:43
  174.3 3.1 fusion.7
  177.5 0.0 copy-start.1
  177.5 0.0 all-reduce.3.cloned.1.call-update
  177.5 0.0 all-reduce.5.cloned.1.call-start
  177.5 254.9 %all-reduce.3.cloned.1.call-done = f32[512,512]{1,0:T(8,128)} async-done(((f32[512,512]{1,0:T(8,128)}), f32[512,512]{1,0:T(8,128)}) %all-reduce.3.cloned.1.call-update) | async-done | bytes 1048592 | tf_op jit(solution)/shard_map/psum | solution.py:20
  432.5 3.9 fusion.2
  436.4 0.0 copy-done.1
  436.4 1.2 convolution_add_fusion.1
  437.6 2.1 fusion.13
  439.7 0.0 all-reduce.5.cloned.1.call-update
  439.7 0.8 copy.9
  440.6 253.9 %all-reduce.5.cloned.1.call-done = f32[512,512]{1,0:T(8,128)} async-done(((f32[512,512]{1,0:T(8,128)}), f32[512,512]{1,0:T(8,128)}) %all-reduce.5.cloned.1.call-update) | async-done | bytes 1048592 | tf_op jit(solution)/shard_map/psum | solution.py:20
  694.4 3.9 fusion.1
  698.3 1.2 fusion.5
  699.6 0.8 copy.10
Async XLA Ops:
  7.2 1.6 copy-start
  7.2 91.1 %reduce-scatter.2.cloned.1.call-start = ((), (), s32[]{:S(2)}) async-start(), calls=%async_computation.1 | async-start | bytes 4456448 | tf_op jit(solution)/shard_map/reduce_scatter | solution.py:31
  12.8 0.9 copy-start.2
  12.8 419.7 %all-reduce.3.cloned.1.call-start = ((), (), s32[]{:S(2)}) async-start(), calls=%async_computation.2 | async-start | bytes 2097152 | tf_op jit(solution)/shard_map/psum | solution.py:20
  177.5 258.9 %copy-start.1 = (f32[128,512]{1,0:T(8,128)S(1)}, f32[128,512]{1,0:T(8,128)}, u32[]{:S(2)}) copy-start(f32[128,512]{1,0:T(8,128)} %reduce-scatter.2.cloned.1.call-done) | copy-start | bytes 786436
  177.5 516.9 %all-reduce.5.cloned.1.call-start = ((), (), s32[]{:S(2)}) async-start(), calls=%async_computation.3 | async-start | bytes 2097152 | tf_op jit(solution)/shard_map/psum | solution.py:20
Sparse Core Ops, SparseCore 0:
  12.9 85.3 reduce-scatter.1
  177.6 254.8 all-reduce.2
  439.9 254.5 all-reduce.4
where the time goes:
time: 707 us
  waiting for transfers between devices  593 us (84%)
  blocking collectives  73.7 us (10%)
  matrix products  19.5 us (3%)
  between operations  14.5 us (2%)
    psum x2, waiting for transfers between devices, gram_total(): return lax.psum(local_gram, ('dp', 'head'))  509 us
    reduce_scatter x1, waiting for transfers between devices, local(): lax.psum_scatter(lax.dot_general(residual, latents, (((0,), (0,)), ((), (...  84.5 us
    psum x1, blocking collectives, local(): squares = lax.psum(jnp.sum(nesterov * nesterov), ('dp', 'head'))  73.7 us
  transfers between devices with their start and end apart: 3, of which 3 were waited for; matrix products, arithmetic and copies ran while one was open for 0% of the time, Pallas kernels for 0%

commit v1 on v0

--- a/solution.py
+++ b/solution.py
@@ -17,7 +17,7 @@
     local_gram = lax.dot_general(
         iterate, iterate, (((1,), (1,)), ((), ())), precision=lax.Precision.HIGHEST
     )
-    return lax.psum(local_gram, ("dp", "head"))
+    return lax.psum(lax.psum(local_gram, "dp"), "head")
 
 
 def local(latents, targets, kv_weight, momentum):

time: 707 us -> 618 us (0.87)
  waiting for transfers between devices: 593 us -> 503 us
    psum x2 -> x4, waiting for transfers between devices: 509 us -> 419 us  [gram_total(): return lax.psum(lax.psum(local_gram, 'dp'), 'head')]
  transfers between devices with their start and end apart: 3 -> 5, of which waited for: 3 -> 5; matrix products, arithmetic and copies ran while one was open for 0% -> 0% of each run, Pallas kernels for 0% -> 0%
where the time goes in v1:
time: 618 us; the launch traced here: 617 us
  waiting for transfers between devices  503 us (81%)
  blocking collectives  73.7 us (12%)
  matrix products  19.9 us (3%)
  between operations  14.6 us (2%)
    psum x4, waiting for transfers between devices, gram_total(): return lax.psum(lax.psum(local_gram, 'dp'), 'head')  419 us
    reduce_scatter x1, waiting for transfers between devices, local(): lax.psum_scatter(lax.dot_general(residual, latents, (((0,), (0,)), ((), (...  84.5 us
    psum x1, blocking collectives, local(): squares = lax.psum(jnp.sum(nesterov * nesterov), ('dp', 'head'))  73.7 us
  transfers between devices with their start and end apart: 5, of which 5 were waited for; matrix products, arithmetic and copies ran while one was open for 0% of the time, Pallas kernels for 0%

profile of v1, /device:TPU:2, one launch (start us, length us, event | category | flops | bytes accessed | tf_op | source)
XLA Modules:
  0.0 617.3 jit_solution(1752516662442821504)
XLA Ops:
  7.2 0.0 copy-start
  7.2 0.0 reduce-scatter.2.cloned.1.call-start
  7.2 1.5 copy-done
  8.8 4.0 fusion.3
  12.8 0.0 copy-start.2
  12.8 0.0 reduce-scatter.2.cloned.1.call-update
  12.8 0.0 all-reduce.5.cloned.1.call-start
  12.9 0.9 copy-done.2
  13.7 0.1 copy.6
  13.9 84.5 %reduce-scatter.2.cloned.1.call-done = f32[128,512]{1,0:T(8,128)} async-done(((f32[2048,512]{1,0:T(8,128)}), f32[128,512]{1,0:T(8,128)}) %reduce-scatter.2.cloned.1.call-update) | async-done | bytes 262160 | tf_op jit(solution)/shard_map/reduce_scatter | solution.py:31
  98.3 1.6 multiply_reduce_fusion
  99.9 73.7 %psum.35 = f32[]{:T(128)} all-reduce(f32[]{:T(128)} %get-tuple-element.4), channel_id=1, replica_groups=mesh['dp'=16,'head'=16] {'dp','head'}, use_global_device_ids=true, to_apply=%region_2.0 | all-reduce | flops 1 | bytes 8 | tf_op jit(solution)/shard_map/psum | solution.py:43
  174.3 3.1 fusion.7
  177.5 0.0 all-reduce.5.cloned.1.call-update
  177.5 0.0 all-reduce.7.cloned.1.call-start
  177.5 95.6 %all-reduce.5.cloned.1.call-done = f32[512,512]{1,0:T(8,128)} async-done(((f32[512,512]{1,0:T(8,128)}), f32[512,512]{1,0:T(8,128)}) %all-reduce.5.cloned.1.call-update) | async-done | bytes 1048592 | tf_op jit(solution)/shard_map/psum | solution.py:20
  273.2 0.0 all-reduce.7.cloned.1.call-update
  273.2 0.0 all-reduce.9.cloned.1.call-start
  273.2 113.5 %all-reduce.7.cloned.1.call-done = f32[512,512]{1,0:T(8,128)} async-done(((f32[512,512]{1,0:T(8,128)}), f32[512,512]{1,0:T(8,128)}) %all-reduce.7.cloned.1.call-update) | async-done | bytes 1048592 | tf_op jit(solution)/shard_map/psum | solution.py:20
  386.8 4.1 fusion.2
  390.9 0.0 copy-done.1
  390.9 1.2 convolution_add_fusion.1
  392.1 2.1 fusion.13
  394.2 0.0 all-reduce.9.cloned.1.call-update
  394.2 0.0 all-reduce.11.cloned.1.call-start
  394.2 97.0 %all-reduce.9.cloned.1.call-done = f32[512,512]{1,0:T(8,128)} async-done(((f32[512,512]{1,0:T(8,128)}), f32[512,512]{1,0:T(8,128)}) %all-reduce.9.cloned.1.call-update) | async-done | bytes 1048592 | tf_op jit(solution)/shard_map/psum | solution.py:20
  491.3 0.0 all-reduce.11.cloned.1.call-update
  491.3 0.8 copy.9
  492.1 112.4 %all-reduce.11.cloned.1.call-done = f32[512,512]{1,0:T(8,128)} async-done(((f32[512,512]{1,0:T(8,128)}), f32[512,512]{1,0:T(8,128)}) %all-reduce.11.cloned.1.call-update) | async-done | bytes 1048592 | tf_op jit(solution)/shard_map/psum | solution.py:20
  604.6 4.1 fusion.1
  608.7 1.2 fusion.5
  609.9 0.8 copy.10
  (1 shorter events, 0.0 us)
Async XLA Ops:
  7.2 1.6 copy-start
  7.2 91.1 %reduce-scatter.2.cloned.1.call-start = ((), (), s32[]{:S(2)}) async-start(), calls=%async_computation.1 | async-start | bytes 4456448 | tf_op jit(solution)/shard_map/reduce_scatter | solution.py:31
  12.8 0.9 copy-start.2
  12.8 260.4 %all-reduce.5.cloned.1.call-start = ((), (), s32[]{:S(2)}) async-start(), calls=%async_computation.2 | async-start | bytes 2097152 | tf_op jit(solution)/shard_map/psum | solution.py:20
  177.5 209.3 %all-reduce.7.cloned.1.call-start = ((), (), s32[]{:S(2)}) async-start(), calls=%async_computation.3 | async-start | bytes 2097152 | tf_op jit(solution)/shard_map/psum | solution.py:20
  273.2 117.7 %copy-start.1 = (f32[128,512]{1,0:T(8,128)S(1)}, f32[128,512]{1,0:T(8,128)}, u32[]{:S(2)}) copy-start(f32[128,512]{1,0:T(8,128)} %reduce-scatter.2.cloned.1.call-done) | copy-start | bytes 786436
  273.2 218.1 %all-reduce.9.cloned.1.call-start = ((), (), s32[]{:S(2)}) async-start(), calls=%async_computation.4 | async-start | bytes 2097152 | tf_op jit(solution)/shard_map/psum | solution.py:20
  394.2 210.4 %all-reduce.11.cloned.1.call-start = ((), (), s32[]{:S(2)}) async-start(), calls=%async_computation.5 | async-start | bytes 2097152 | tf_op jit(solution)/shard_map/psum | solution.py:20
Sparse Core Ops, SparseCore 0:
  12.9 85.3 reduce-scatter.1
  177.6 95.5 all-reduce.4
  275.6 111.0 all-reduce.6
  394.3 96.9 all-reduce.8
  493.5 111.0 all-reduce.10
